TPU v7x, 256 devices: a whole 4x4x8 slice. The times are simulated.
256 devices in a mesh: panel: 16 (over z, core), tm: 16 (over x, y).
Axes of the slice: x: 4, y: 4, z: 8, core: 2. Of those that a mesh axis runs over, the one named last changes fastest.
Arguments:
- pressures: bfloat16 [98304, 12288], P('panel', 'tm'), may hold values from -60 to 60
- sketch: bfloat16 [98304, 128], P(('panel', 'tm')), may hold values from -6 to 6
Outputs:
- basis_rows: bfloat16 [12288, 128], P('tm')
- image: float32 [98304, 128], P(('panel', 'tm'))
All inputs are finite; a program needn't handle non-finite values.
Results may differ from a plain program's by a relative error of at most 0.0029.
Values may be sent and summed in bfloat16 or wider, within the bound.
No kernel may reach another device: no remote copies, remote signals or barrier semaphores. Data moves between devices by JAX's collectives and lax.ppermute only.
A program may use at most 64 MiB of HBM per device.

v0:
```python
import jax
import jax.numpy as jnp
from jax import lax
from jax.sharding import PartitionSpec as P


def gram_of(rows_block):
    return lax.dot_general(
        rows_block,
        rows_block,
        (((0,), (0,)), ((), ())),
        precision=lax.Precision.HIGHEST,
        preferred_element_type=jnp.float32,
    )


def orthonormal(rows_block, gram_matrix):
    lower_factor = jnp.linalg.cholesky(gram_matrix)
    solved = jax.scipy.linalg.solve_triangular(lower_factor, rows_block.T, lower=True)
    return solved.T.astype(jnp.bfloat16)


def on_device(pressures, sketch):
    partial_y = lax.dot_general(
        pressures,
        lax.all_gather(sketch, "tm", axis=0, tiled=True),
        (((0,), (0,)), ((), ())),
        preferred_element_type=jnp.float32,
    )
    y_rows = lax.psum(partial_y, "panel")
    gram_matrix = lax.psum(gram_of(y_rows), "tm")
    basis_rows = orthonormal(y_rows, gram_matrix)
    own_rows = pressures.shape[0] // lax.axis_size("tm")
    full_image = lax.psum(jnp.dot(pressures, basis_rows, preferred_element_type=jnp.float32), "tm")
    image = lax.dynamic_slice_in_dim(full_image, lax.axis_index("tm") * own_rows, own_rows, 0)
    return (basis_rows, image)


def solution(mesh):
    return jax.shard_map(
        on_device,
        mesh=mesh,
        in_specs=(P("panel", "tm"), P(("panel", "tm"), None)),
        out_specs=(P("tm", None), P(("panel", "tm"), None)),
        check_vma=False,
    )
```

profile of v0, /device:TPU:1, one launch (start us, length us, event | category | flops | bytes accessed | tf_op | source)
XLA Modules:
  0.0 423.2 jit_solution(15949933175070414837)
XLA Ops:
  7.2 0.0 all-gather.2.cloned.1.call-start
  7.2 0.7 all-gather.2.cloned.1.call-update
  7.9 0.0 all-reduce.4.cloned.1.call-start
  7.9 54.4 %all-gather.2.cloned.1.call-done = bf16[6144,128]{1,0:T(8,128)(2,1)} async-done(((bf16[384,128]{1,0:T(8,128)(2,1)}), bf16[6144,128]{1,0:T(8,128)(2,1)}) %all-gather.2.cloned.1.call-update) | async-done | bytes 1572880 | tf_op jit(solution)/shard_map/all_gather | solution.py:26
  62.3 7.5 %fusion.3 = f32[768,128]{1,0:T(8,128)} fusion(bf16[6144,768]{1,0:T(8,128)(2,1)} %param.2, bf16[6144,128]{1,0:T(8,128)(2,1)} %all-gather.2.cloned.1.call-done), kind=kOutput, calls=%fused_computation.12 | convolution fusion | flops 1207959552 | bytes 11403264 | tf_op jit(solution)/shard_map/dot_general | solution.py:24
  69.8 0.0 all-reduce.4.cloned.1.call-update
  69.8 0.0 all-reduce.6.cloned.1.call-start
  69.9 109.7 %all-reduce.4.cloned.1.call-done = f32[768,128]{1,0:T(8,128)} async-done(((f32[768,128]{1,0:T(8,128)}), f32[768,128]{1,0:T(8,128)}) %all-reduce.4.cloned.1.call-update) | async-done | bytes 393232 | tf_op jit(solution)/shard_map/psum | solution.py:30
  179.6 2.5 fusion.4
  182.1 0.0 all-reduce.6.cloned.1.call-update
  182.2 0.2 all-reduce.8.cloned.1.call-start
  182.4 91.2 %all-reduce.6.cloned.1.call-done = f32[128,128]{0,1:T(8,128)} async-done(((f32[128,128]{0,1:T(8,128)}), f32[128,128]{0,1:T(8,128)}) %all-reduce.6.cloned.1.call-update) | async-done | bytes 65552 | tf_op jit(solution)/shard_map/psum | solution.py:31
  273.5 0.9 copy.5
  274.5 0.9 fusion.2
  275.3 11.7 %cholesky.16 = f32[128,128]{1,0:T(8,128)S(1)} custom-call(f32[128,128]{1,0:T(8,128)S(1)} %fusion.2), custom_call_target="Cholesky" | custom-call | tf_op jit(solution)/shard_map/jit(cholesky)/cholesky | solution.py:18
  287.1 0.6 compare_reduce_fusion
  287.7 0.7 fusion
  288.4 9.8 %custom-call.7 = f32[1,128,128]{1,2,0:T(8,128)S(1)} custom-call(f32[1,128,128]{2,1,0:T(8,128)S(1)} %fusion), custom_call_target="InvertDiagBlocksLowerTriangular" | custom-call | tf_op jit(solution)/shard_map/jit(_solve_triangular)/triangular_solve | solution.py:19
  298.2 1.5 convolution_convert_fusion
  299.7 8.7 %convolution_bitcast_fusion = f32[6144,128]{0,1:T(8,128)} fusion(bf16[768,128]{1,0:T(8,128)(2,1)S(1)} %convolution_convert_fusion, bf16[6144,768]{1,0:T(8,128)(2,1)} %param.2), kind=kOutput, calls=%fused_computation | convolution fusion | flops 1207959552 | bytes 12779520 | tf_op jit(solution)/shard_map/dot_general | solution.py:34
  308.3 0.0 all-reduce.8.cloned.1.call-update
  308.4 106.5 %all-reduce.8.cloned.1.call-done = f32[6144,128]{0,1:T(8,128)} async-done(((f32[6144,128]{0,1:T(8,128)}), f32[6144,128]{0,1:T(8,128)}) %all-reduce.8.cloned.1.call-update) | async-done | bytes 3145744 | tf_op jit(solution)/shard_map/psum | solution.py:34
  414.9 0.9 constant_dynamic-slice_fusion
  415.8 0.8 copy.6
  (3 shorter events, 0.0 us)
Async XLA Ops:
  7.2 55.2 %all-gather.2.cloned.1.call-start = ((), (), s32[]{:S(2)}) async-start(), calls=%async_computation | async-start | bytes 1671168 | tf_op jit(solution)/shard_map/all_gather | solution.py:26
  7.9 171.7 %all-reduce.4.cloned.1.call-start = ((), (), s32[]{:S(2)}) async-start(), calls=%async_computation.1 | async-start | bytes 786432 | tf_op jit(solution)/shard_map/psum | solution.py:30
  69.8 203.7 %all-reduce.6.cloned.1.call-start = ((), (), s32[]{:S(2)}) async-start(), calls=%async_computation.2 | async-start | bytes 131072 | tf_op jit(solution)/shard_map/psum | solution.py:31
  182.2 232.8 %all-reduce.8.cloned.1.call-start = ((), (), s32[]{:S(2)}) async-start(), calls=%async_computation.3 | async-start | bytes 6291456 | tf_op jit(solution)/shard_map/psum | solution.py:34
  299.7 8.7 %copy-start = (bf16[768,128]{1,0:T(8,128)(2,1)}, bf16[768,128]{1,0:T(8,128)(2,1)S(1)}, u32[]{:S(2)}) copy-start(bf16[768,128]{1,0:T(8,128)(2,1)S(1)} %convolution_convert_fusion) | copy-start | bytes 589828
Sparse Core Ops, SparseCore 0:
  10.5 51.7 all-gather.1
  69.9 109.6 all-reduce.3
  183.7 89.8 all-reduce.5
  308.5 106.3 all-reduce.7
where the time goes:
time: 424 us; the launch traced here: 423 us
  waiting for transfers between devices  363 us (86%)
  other arithmetic  23.7 us (6%)
  matrix products  20.1 us (5%)
  between operations  13.8 us (3%)
    psum x1, waiting for transfers between devices, on_device(): y_rows = lax.psum(partial_y, 'panel')  110 us
    psum x1, waiting for transfers between devices, on_device(): lax.psum(jnp.dot(pressures, basis_rows, preferred_element_type=jnp.float3...  107 us
    psum x1, waiting for transfers between devices, on_device(): gram_matrix = lax.psum(gram_of(y_rows), 'tm')  91.2 us
    all_gather x1, waiting for transfers between devices, on_device(): lax.all_gather(sketch, 'tm', axis=0, tiled=True)  54.4 us
    another operation x3, other arithmetic, orthonormal(): lower_factor = jnp.linalg.cholesky(gram_matrix)  12.4 us
    another operation x2, other arithmetic, orthonormal(): jax.scipy.linalg.solve_triangular(lower_factor, rows_block.T, lower=True)  10.5 us
    dot_general x1, matrix products, on_device(): jnp.dot(pressures, basis_rows, preferred_element_type=jnp.float32)  8.66 us
  transfers between devices with their start and end apart: 4, of which 4 were waited for; matrix products, arithmetic and copies ran while one was open for 0% of the time, Pallas kernels for 0%

commit v1 on v0

--- a/solution.py
+++ b/solution.py
@@ -2,6 +2,13 @@
 import jax.numpy as jnp
 from jax import lax
 from jax.sharding import PartitionSpec as P
+
+
+def exchange_gather(x, name, d):
+    size = lax.axis_size(name)
+    blocks = jnp.stack([x for _ in range(size)])
+    blocks = lax.all_to_all(blocks, name, split_axis=0, concat_axis=0)
+    return jnp.concatenate(blocks, axis=d)
 
 
 def gram_of(rows_block):
@@ -23,7 +30,7 @@
 def on_device(pressures, sketch):
     partial_y = lax.dot_general(
         pressures,
-        lax.all_gather(sketch, "tm", axis=0, tiled=True),
+        exchange_gather(sketch, "tm", 0),
         (((0,), (0,)), ((), ())),
         preferred_element_type=jnp.float32,
     )

time: 424 us -> 399 us (0.941)
  waiting for transfers between devices: 363 us -> 308 us
  blocking collectives: 0 us -> 28.9 us
    all_gather x1 -> x0, waiting for transfers between devices: 54.4 us -> none  [on_device(): lax.all_gather(sketch, 'tm', axis=0, tiled=True)]
    all_to_all x0 -> x1, blocking collectives: none -> 28.9 us  [exchange_gather(): blocks = lax.all_to_all(blocks, name, split_axis=0, concat_axis=0)]
  transfers between devices with their start and end apart: 4 -> 3, of which waited for: 4 -> 3; matrix products, arithmetic and copies ran while one was open for 0% -> 0% of each run, Pallas kernels for 0% -> 0%
where the time goes in v1:
time: 399 us; the launch traced here: 398 us
  waiting for transfers between devices  308 us (77%)
  blocking collectives  28.9 us (7%)
  other arithmetic  23.7 us (6%)
  matrix products  19.7 us (5%)
  between operations  13.8 us (3%)
    psum x1, waiting for transfers between devices, on_device(): y_rows = lax.psum(partial_y, 'panel')  110 us
    psum x1, waiting for transfers between devices, on_device(): lax.psum(jnp.dot(pressures, basis_rows, preferred_element_type=jnp.float3...  107 us
    psum x1, waiting for transfers between devices, on_device(): gram_matrix = lax.psum(gram_of(y_rows), 'tm')  91.1 us
    all_to_all x1, blocking collectives, exchange_gather(): blocks = lax.all_to_all(blocks, name, split_axis=0, concat_axis=0)  28.9 us
    another operation x3, other arithmetic, orthonormal(): lower_factor = jnp.linalg.cholesky(gram_matrix)  12.4 us
    another operation x2, other arithmetic, orthonormal(): jax.scipy.linalg.solve_triangular(lower_factor, rows_block.T, lower=True)  10.5 us
    dot_general x1, matrix products, on_device(): jnp.dot(pressures, basis_rows, preferred_element_type=jnp.float32)  8.66 us
  transfers between devices with their start and end apart: 3, of which 3 were waited for; matrix products, arithmetic and copies ran while one was open for 0% of the time, Pallas kernels for 0%

profile of v1, /device:TPU:1, one launch (start us, length us, event | category | flops | bytes accessed | tf_op | source)
XLA Modules:
  0.0 398.5 jit_solution(15951695205928496795)
XLA Ops:
  7.2 0.0 all-reduce.4.cloned.1.call-start
  7.2 1.2 stack.2
  8.4 28.9 %all_to_all.5 = bf16[16,384,128]{2,1,0:T(8,128)(2,1)S(1)} all-to-all(bf16[16,384,128]{2,1,0:T(8,128)(2,1)S(1)} %stack.2), channel_id=1, replica_groups=mesh['panel'=16,'tm'=16] {'tm'}, dimensions={0} | all-to-all | bytes 3145728 | tf_op jit(solution)/shard_map/all_to_all | solution.py:10
  37.3 7.1 %fusion.3 = f32[768,128]{1,0:T(8,128)} fusion(bf16[6144,768]{1,0:T(8,128)(2,1)} %param.2, bf16[6144,128]{1,0:T(8,128)(2,1)S(1)} %bitcast.19), kind=kOutput, calls=%fused_computation.12 | convolution fusion | flops 1207959552 | bytes 11403264 | tf_op jit(solution)/shard_map/dot_general | solution.py:31
  44.4 0.0 all-reduce.4.cloned.1.call-update
  44.4 0.0 all-reduce.6.cloned.1.call-start
  44.4 110.5 %all-reduce.4.cloned.1.call-done = f32[768,128]{1,0:T(8,128)} async-done(((f32[768,128]{1,0:T(8,128)}), f32[768,128]{1,0:T(8,128)}) %all-reduce.4.cloned.1.call-update) | async-done | bytes 393232 | tf_op jit(solution)/shard_map/psum | solution.py:37
  154.9 2.5 fusion.4
  157.4 0.0 all-reduce.6.cloned.1.call-update
  157.5 0.2 all-reduce.8.cloned.1.call-start
  157.7 91.1 %all-reduce.6.cloned.1.call-done = f32[128,128]{0,1:T(8,128)} async-done(((f32[128,128]{0,1:T(8,128)}), f32[128,128]{0,1:T(8,128)}) %all-reduce.6.cloned.1.call-update) | async-done | bytes 65552 | tf_op jit(solution)/shard_map/psum | solution.py:38
  248.8 0.9 copy.5
  249.8 0.9 fusion.2
  250.6 11.7 %cholesky.16 = f32[128,128]{1,0:T(8,128)S(1)} custom-call(f32[128,128]{1,0:T(8,128)S(1)} %fusion.2), custom_call_target="Cholesky" | custom-call | tf_op jit(solution)/shard_map/jit(cholesky)/cholesky | solution.py:25
  262.4 0.6 compare_reduce_fusion
  263.0 0.7 fusion
  263.7 9.8 %custom-call.7 = f32[1,128,128]{1,2,0:T(8,128)S(1)} custom-call(f32[1,128,128]{2,1,0:T(8,128)S(1)} %fusion), custom_call_target="InvertDiagBlocksLowerTriangular" | custom-call | tf_op jit(solution)/shard_map/jit(_solve_triangular)/triangular_solve | solution.py:26
  273.5 1.5 convolution_convert_fusion
  275.0 0.0 copy-start
  275.0 8.7 %convolution_bitcast_fusion = f32[6144,128]{0,1:T(8,128)} fusion(bf16[768,128]{1,0:T(8,128)(2,1)S(1)} %convolution_convert_fusion, bf16[6144,768]{1,0:T(8,128)(2,1)} %param.2), kind=kOutput, calls=%fused_computation | convolution fusion | flops 1207959552 | bytes 12779520 | tf_op jit(solution)/shard_map/dot_general | solution.py:41
  283.6 0.0 all-reduce.8.cloned.1.call-update
  283.7 106.5 %all-reduce.8.cloned.1.call-done = f32[6144,128]{0,1:T(8,128)} async-done(((f32[6144,128]{0,1:T(8,128)}), f32[6144,128]{0,1:T(8,128)}) %all-reduce.8.cloned.1.call-update) | async-done | bytes 3145744 | tf_op jit(solution)/shard_map/psum | solution.py:41
  390.2 0.9 constant_dynamic-slice_fusion
  391.2 0.8 copy.6
  (2 shorter events, 0.0 us)
Async XLA Ops:
  7.2 147.7 %all-reduce.4.cloned.1.call-start = ((), (), s32[]{:S(2)}) async-start(), calls=%async_computation.1 | async-start | bytes 786432 | tf_op jit(solution)/shard_map/psum | solution.py:37
  44.4 204.5 %all-reduce.6.cloned.1.call-start = ((), (), s32[]{:S(2)}) async-start(), calls=%async_computation.2 | async-start | bytes 131072 | tf_op jit(solution)/shard_map/psum | solution.py:38
  157.5 232.7 %all-reduce.8.cloned.1.call-start = ((), (), s32[]{:S(2)}) async-start(), calls=%async_computation.3 | async-start | bytes 6291456 | tf_op jit(solution)/shard_map/psum | solution.py:41
  275.0 8.7 %copy-start = (bf16[768,128]{1,0:T(8,128)(2,1)}, bf16[768,128]{1,0:T(8,128)(2,1)S(1)}, u32[]{:S(2)}) copy-start(bf16[768,128]{1,0:T(8,128)(2,1)S(1)} %convolution_convert_fusion) | copy-start | bytes 589828
Sparse Core Ops, SparseCore 0:
  44.5 110.3 all-reduce.3
  159.0 89.8 all-reduce.5
  283.8 106.3 all-reduce.7

commit v2 on v0

--- a/solution.py
+++ b/solution.py
@@ -2,6 +2,7 @@
 import jax.numpy as jnp
 from jax import lax
 from jax.sharding import PartitionSpec as P
+from jax.lax import all_gather
 
 
 def gram_of(rows_block):
@@ -28,7 +29,8 @@
         preferred_element_type=jnp.float32,
     )
     y_rows = lax.psum(partial_y, "panel")
-    gram_matrix = lax.psum(gram_of(y_rows), "tm")
+    arr = gram_of(y_rows)
+    gram_matrix = all_gather(arr, "tm").sum(axis=0)
     basis_rows = orthonormal(y_rows, gram_matrix)
     own_rows = pressures.shape[0] // lax.axis_size("tm")
     full_image = lax.psum(jnp.dot(pressures, basis_rows, preferred_element_type=jnp.float32), "tm")

time: 424 us -> 379 us (0.89)
  waiting for transfers between devices: 363 us -> 318 us
    psum x1 -> x0, waiting for transfers between devices: 91.2 us -> none  [on_device(): gram_matrix = lax.psum(gram_of(y_rows), 'tm')]
    all_gather x0 -> x1, waiting for transfers between devices: none -> 47.2 us  [on_device(): gram_matrix = all_gather(arr, 'tm').sum(axis=0)]
where the time goes in v2:
time: 379 us
  waiting for transfers between devices  318 us (84%)
  other arithmetic  24.1 us (6%)
  matrix products  20.1 us (5%)
  between operations  13.8 us (4%)
    psum x1, waiting for transfers between devices, on_device(): y_rows = lax.psum(partial_y, 'panel')  110 us
    psum x1, waiting for transfers between devices, on_device(): lax.psum(jnp.dot(pressures, basis_rows, preferred_element_type=jnp.float3...  106 us
    all_gather x1, waiting for transfers between devices, on_device(): lax.all_gather(sketch, 'tm', axis=0, tiled=True)  54.4 us
    all_gather x1, waiting for transfers between devices, on_device(): gram_matrix = all_gather(arr, 'tm').sum(axis=0)  47.2 us
    another operation x3, other arithmetic, orthonormal(): lower_factor = jnp.linalg.cholesky(gram_matrix)  12.4 us
    another operation x2, other arithmetic, orthonormal(): jax.scipy.linalg.solve_triangular(lower_factor, rows_block.T, lower=True)  10.5 us
    dot_general x1, matrix products, on_device(): jnp.dot(pressures, basis_rows, preferred_element_type=jnp.float32)  8.65 us
  transfers between devices with their start and end apart: 4, of which 4 were waited for; matrix products, arithmetic and copies ran while one was open for 0% of the time, Pallas kernels for 0%

profile of v2, /device:TPU:1, one launch (start us, length us, event | category | flops | bytes accessed | tf_op | source)
XLA Modules:
  0.0 378.6 jit_solution(1641575515055281031)
XLA Ops:
  7.2 0.0 all-gather.4.cloned.1.call-start
  7.2 0.7 all-gather.4.cloned.1.call-update
  7.9 0.0 all-reduce.3.cloned.1.call-start
  7.9 54.4 %all-gather.4.cloned.1.call-done = bf16[6144,128]{1,0:T(8,128)(2,1)} async-done(((bf16[384,128]{1,0:T(8,128)(2,1)}), bf16[6144,128]{1,0:T(8,128)(2,1)}) %all-gather.4.cloned.1.call-update) | async-done | bytes 1572880 | tf_op jit(solution)/shard_map/all_gather | solution.py:27
  62.3 7.5 %fusion.3 = f32[768,128]{1,0:T(8,128)} fusion(bf16[6144,768]{1,0:T(8,128)(2,1)} %param.2, bf16[6144,128]{1,0:T(8,128)(2,1)} %all-gather.4.cloned.1.call-done), kind=kOutput, calls=%fused_computation.12 | convolution fusion | flops 1207959552 | bytes 11403264 | tf_op jit(solution)/shard_map/dot_general | solution.py:25
  69.8 0.0 all-reduce.3.cloned.1.call-update
  69.8 0.0 all-gather.6.cloned.1.call-start
  69.9 109.7 %all-reduce.3.cloned.1.call-done = f32[768,128]{1,0:T(8,128)} async-done(((f32[768,128]{1,0:T(8,128)}), f32[768,128]{1,0:T(8,128)}) %all-reduce.3.cloned.1.call-update) | async-done | bytes 393232 | tf_op jit(solution)/shard_map/psum | solution.py:31
  179.6 2.5 fusion.4
  182.1 0.0 all-gather.6.cloned.1.call-update
  182.2 0.2 all-reduce.5.cloned.1.call-start
  182.4 47.2 %all-gather.6.cloned.1.call-done = f32[2048,128]{1,0:T(8,128)} async-done(((f32[128,128]{1,0:T(8,128)}), f32[2048,128]{1,0:T(8,128)}) %all-gather.6.cloned.1.call-update) | async-done | bytes 1048592 | tf_op jit(solution)/shard_map/all_gather | solution.py:33
  229.6 1.3 reduce_sum.9
  230.9 0.1 copy.6
  231.0 11.7 %cholesky.16 = f32[128,128]{1,0:T(8,128)S(1)} custom-call(f32[128,128]{1,0:T(8,128)S(1)} %fusion.2), custom_call_target="Cholesky" | custom-call | tf_op jit(solution)/shard_map/jit(cholesky)/cholesky | solution.py:19
  242.7 0.6 compare_reduce_fusion
  243.4 0.7 fusion
  244.0 9.8 %custom-call.7 = f32[1,128,128]{1,2,0:T(8,128)S(1)} custom-call(f32[1,128,128]{2,1,0:T(8,128)S(1)} %fusion), custom_call_target="InvertDiagBlocksLowerTriangular" | custom-call | tf_op jit(solution)/shard_map/jit(_solve_triangular)/triangular_solve | solution.py:20
  253.9 1.5 convolution_convert_fusion
  255.3 8.7 %convolution_bitcast_fusion = f32[6144,128]{0,1:T(8,128)} fusion(bf16[768,128]{1,0:T(8,128)(2,1)S(1)} %convolution_convert_fusion, bf16[6144,768]{1,0:T(8,128)(2,1)} %param.2), kind=kOutput, calls=%fused_computation | convolution fusion | flops 1207959552 | bytes 12779520 | tf_op jit(solution)/shard_map/dot_general | solution.py:36
  264.0 0.0 all-reduce.5.cloned.1.call-update
  264.0 106.3 %all-reduce.5.cloned.1.call-done = f32[6144,128]{0,1:T(8,128)} async-done(((f32[6144,128]{0,1:T(8,128)}), f32[6144,128]{0,1:T(8,128)}) %all-reduce.5.cloned.1.call-update) | async-done | bytes 3145744 | tf_op jit(solution)/shard_map/psum | solution.py:36
  370.3 0.9 constant_dynamic-slice_fusion
  371.3 0.8 copy.7
  (4 shorter events, 0.1 us)
Async XLA Ops:
  7.2 55.2 %all-gather.4.cloned.1.call-start = ((), (), s32[]{:S(2)}) async-start(), calls=%async_computation | async-start | bytes 1671168 | tf_op jit(solution)/shard_map/all_gather | solution.py:27
  7.9 171.7 %all-reduce.3.cloned.1.call-start = ((), (), s32[]{:S(2)}) async-start(), calls=%async_computation.1 | async-start | bytes 786432 | tf_op jit(solution)/shard_map/psum | solution.py:31
  69.8 159.8 %all-gather.6.cloned.1.call-start = ((), (), s32[]{:S(2)}) async-start(), calls=%async_computation.3 | async-start | bytes 1114112 | tf_op jit(solution)/shard_map/all_gather | solution.py:33
  182.2 188.2 %all-reduce.5.cloned.1.call-start = ((), (), s32[]{:S(2)}) async-start(), calls=%async_computation.2 | async-start | bytes 6291456 | tf_op jit(solution)/shard_map/psum | solution.py:36
  255.3 8.7 %copy-start = (bf16[768,128]{1,0:T(8,128)(2,1)}, bf16[768,128]{1,0:T(8,128)(2,1)S(1)}, u32[]{:S(2)}) copy-start(bf16[768,128]{1,0:T(8,128)(2,1)S(1)} %convolution_convert_fusion) | copy-start | bytes 589828
Sparse Core Ops, SparseCore 0:
  10.5 51.7 all-gather.3
  69.9 109.6 all-reduce.2
  182.9 46.6 all-gather.5
  264.1 106.1 all-reduce.4
